TPU v7x, 256 devices: a whole 4x4x8 slice. The times are simulated.
256 devices in a mesh: site: 2 (over core), wide: 32 (over x, z), narrow: 4 (over y).
Axes of the slice: x: 4, y: 4, z: 8, core: 2. Of those that a mesh axis runs over, the one named last changes fastest.
Arguments:
- initial_rows: float32 [64, 4, 2048], P('site', 'narrow'), may hold values from -6 to 6
- outcomes: int32 [64, 4], replicated, may hold values 0 or 1
- tensors: float32 [4, 2, 4, 2048, 8192], P('site', None, 'narrow', None, 'wide'), may hold values from -0.25 to 0.25
Outputs:
- final_rows: float32 [64, 4, 2048], P('site', 'narrow')
- log_weight: float32 [64], P('site')
All inputs are finite; a program needn't handle non-finite values.
Results may differ from a plain program's by a relative error of at most 0.0003.
Values sent between devices are 32-bit elements; how exact they have to be, the bound alone decides.
A program may use at most 64 MiB of HBM per device.

v0:
```python
import jax
import jax.numpy as jnp
from jax import lax
from jax.sharding import PartitionSpec as P

BOND = 8192
epsilon = 1e-06
highest = lax.Precision.HIGHEST


def from_partner(value, axis, distance):
    mask = 2**distance
    pairs = [(source, source ^ mask) for source in range(lax.axis_size(axis))]
    return lax.ppermute(value, axis, pairs)


def advance(held, log_sum, site_tensor, chosen):
    front = held.shape[0]
    groups = lax.axis_size("narrow")
    share = front // groups
    summed = lax.psum_scatter(
        jnp.einsum(
            "bar,oard->bod",
            held,
            site_tensor,
            precision=highest,
            preferred_element_type=jnp.float32,
        ),
        "narrow",
        scatter_dimension=0,
        tiled=True,
    )
    local_choice = lax.dynamic_slice_in_dim(chosen, lax.axis_index("narrow") * share, share, 0)
    squares = jnp.sum(summed * summed, axis=2)
    raw_kept = jnp.where(local_choice[:, None] == 0, summed[:, 0, :], summed[:, 1, :])
    totals = lax.psum(squares, "wide")
    both_mean = (totals[:, 0] + totals[:, 1]) / (2.0 * BOND)
    scale = lax.rsqrt(both_mean + epsilon)
    full_rows = lax.all_gather(raw_kept * scale[:, None], "wide", axis=1, tiled=True)
    kept_square = jnp.where(local_choice == 0, totals[:, 0], totals[:, 1])
    local_ratio = jnp.log(kept_square / BOND + epsilon) - jnp.log(both_mean + epsilon)
    ratio_table = jnp.broadcast_to(local_ratio[:, None], (share, groups))
    split_rows = full_rows.reshape(share, groups, -1)
    moved, moved_ratio = (
        lax.all_to_all(split_rows, "narrow", split_axis=1, concat_axis=0, tiled=True),
        lax.all_to_all(ratio_table, "narrow", split_axis=1, concat_axis=0, tiled=True),
    )
    return (moved, log_sum + moved_ratio[:, 0])


def run_section(held, log_sum, tensors, chosen_block):
    for local_site in range(tensors.shape[0]):
        held, log_sum = advance(held, log_sum, tensors[local_site], chosen_block[:, local_site])
    return (held, log_sum)


def hand_over(held, log_sum):
    moved_rows, moved_sum = from_partner((held, log_sum), "site", 0)
    return (moved_rows, moved_sum)


def shards(initial_rows, outcomes, tensors):
    section = lax.axis_index("site")
    front = initial_rows.shape[0]
    local_count = tensors.shape[0]
    section_columns = lax.dynamic_slice_in_dim(outcomes, section * local_count, local_count, 1)
    held = initial_rows
    log_sum = jnp.zeros((front,), jnp.float32)
    front_order = (section, 1 - section, section)
    for turn_index in range(3):
        new_rows, new_sum = run_section(
            held,
            log_sum,
            tensors,
            lax.dynamic_slice_in_dim(section_columns, front_order[turn_index] * front, front, 0),
        )
        if turn_index == 1:
            held, log_sum = (new_rows, new_sum)
        else:
            active = section == 0 if turn_index == 0 else section == 1
            held = jnp.where(active, new_rows, held)
            log_sum = jnp.where(active, new_sum, log_sum)
        if turn_index < 2:
            held, log_sum = hand_over(held, log_sum)
    return (held, log_sum)


def solution(mesh):
    placed = (P("site", "narrow", None), P(), P("site", None, "narrow", None, "wide"))
    return jax.shard_map(
        shards,
        mesh=mesh,
        in_specs=placed,
        out_specs=(P("site", "narrow", None), P("site")),
        check_vma=False,
    )
```

profile of v0, /device:TPU:2, one launch (start us, length us, event | category | flops | bytes accessed | tf_op | source)
XLA Modules:
  0.0 993.4 jit_solution(1777501969221541964)
XLA Ops:
  7.2 5.4 fusion.2
  12.7 0.8 fusion.33
  13.6 25.4 %reduce-scatter.7.cloned.1.call-done = f32[8,2,256]{2,0,1:T(8,128)} async-done(((f32[32,2,256]{2,0,1:T(8,128)}), f32[8,2,256]{2,0,1:T(8,128)}) %reduce-scatter.7.cloned.1.call-update) | async-done | bytes 16400 | tf_op jit(solution)/shard_map/reduce_scatter | solution.py:21
  39.0 0.8 multiply_reduce_fusion.5
  39.8 63.2 %psum.42 = f32[8,2]{0,1:T(2,128)S(1)} all-reduce(f32[8,2]{0,1:T(2,128)S(1)} %multiply_reduce_fusion.5), channel_id=1, replica_groups=mesh['site'=2,'wide'=32,'narrow'=4] {'wide'}, use_global_device_ids=true, to_apply=%region_2.3 | all-reduce | flops 16 | bytes 128 | tf_op jit(solution)/shard_map/psum | solution.py:36
  103.1 0.8 fusion.24
  103.9 58.4 %all_gather.18 = f32[8,8192]{1,0:T(8,128)S(1)} all-gather(f32[8,256]{1,0:T(8,128)S(1)} %fusion.24), channel_id=1, replica_groups=mesh['site'=2,'wide'=32,'narrow'=4] {'wide'}, dimensions={1}, use_global_device_ids=true | all-gather | bytes 270336 | tf_op jit(solution)/shard_map/all_gather | solution.py:39
  162.3 9.2 all_to_all.171
  171.5 5.3 fusion.5
  176.9 18.2 %reduce-scatter.9.cloned.1.call-done = f32[8,2,256]{2,0,1:T(8,128)} async-done(((f32[32,2,256]{2,0,1:T(8,128)}), f32[8,2,256]{2,0,1:T(8,128)}) %reduce-scatter.9.cloned.1.call-update) | async-done | bytes 16400 | tf_op jit(solution)/shard_map/reduce_scatter | solution.py:21
  195.0 0.8 multiply_reduce_fusion.4
  195.9 63.2 %psum.43 = f32[8,2]{0,1:T(2,128)S(1)} all-reduce(f32[8,2]{0,1:T(2,128)S(1)} %multiply_reduce_fusion.4), channel_id=1, replica_groups=mesh['site'=2,'wide'=32,'narrow'=4] {'wide'}, use_global_device_ids=true, to_apply=%region_5.6 | all-reduce | flops 16 | bytes 128 | tf_op jit(solution)/shard_map/psum | solution.py:36
  259.2 0.8 fusion.22
  260.0 62.4 %all_gather.19 = f32[8,8192]{1,0:T(8,128)} all-gather(f32[8,256]{1,0:T(8,128)S(1)} %fusion.22), channel_id=1, replica_groups=mesh['site'=2,'wide'=32,'narrow'=4] {'wide'}, dimensions={1}, use_global_device_ids=true | all-gather | bytes 270336 | tf_op jit(solution)/shard_map/all_gather | solution.py:39
  322.4 3.4 all-to-all-start.1
  325.9 6.6 all-to-all-done.1
  332.5 0.1 bitcast_select_fusion.1
  332.7 1.5 collective-permute-done
  334.2 5.3 fusion.1
  339.6 18.2 %reduce-scatter.11.cloned.1.call-done = f32[8,2,256]{2,0,1:T(8,128)} async-done(((f32[32,2,256]{2,0,1:T(8,128)}), f32[8,2,256]{2,0,1:T(8,128)}) %reduce-scatter.11.cloned.1.call-update) | async-done | bytes 16400 | tf_op jit(solution)/shard_map/reduce_scatter | solution.py:21
  357.8 0.8 multiply_reduce_fusion.3
  358.6 63.2 %psum.44 = f32[8,2]{0,1:T(2,128)S(1)} all-reduce(f32[8,2]{0,1:T(2,128)S(1)} %multiply_reduce_fusion.3), channel_id=1, replica_groups=mesh['site'=2,'wide'=32,'narrow'=4] {'wide'}, use_global_device_ids=true, to_apply=%region_8.9 | all-reduce | flops 16 | bytes 128 | tf_op jit(solution)/shard_map/psum | solution.py:36
  422.0 0.8 fusion.20
  422.8 58.4 %all_gather.20 = f32[8,8192]{1,0:T(8,128)S(1)} all-gather(f32[8,256]{1,0:T(8,128)S(1)} %fusion.20), channel_id=1, replica_groups=mesh['site'=2,'wide'=32,'narrow'=4] {'wide'}, dimensions={1}, use_global_device_ids=true | all-gather | bytes 270336 | tf_op jit(solution)/shard_map/all_gather | solution.py:39
  481.1 9.2 all_to_all.172
  490.3 5.3 fusion.4
  495.7 18.1 %reduce-scatter.13.cloned.1.call-done = f32[8,2,256]{2,0,1:T(8,128)} async-done(((f32[32,2,256]{2,0,1:T(8,128)}), f32[8,2,256]{2,0,1:T(8,128)}) %reduce-scatter.13.cloned.1.call-update) | async-done | bytes 16400 | tf_op jit(solution)/shard_map/reduce_scatter | solution.py:21
  513.8 0.8 multiply_reduce_fusion.2
  514.7 63.2 %psum.45 = f32[8,2]{0,1:T(2,128)S(1)} all-reduce(f32[8,2]{0,1:T(2,128)S(1)} %multiply_reduce_fusion.2), channel_id=1, replica_groups=mesh['site'=2,'wide'=32,'narrow'=4] {'wide'}, use_global_device_ids=true, to_apply=%region_11.12 | all-reduce | flops 16 | bytes 128 | tf_op jit(solution)/shard_map/psum | solution.py:36
  578.0 0.8 fusion.18
  578.8 58.4 %all_gather.21 = f32[8,8192]{1,0:T(8,128)S(1)} all-gather(f32[8,256]{1,0:T(8,128)S(1)} %fusion.18), channel_id=1, replica_groups=mesh['site'=2,'wide'=32,'narrow'=4] {'wide'}, dimensions={1}, use_global_device_ids=true | all-gather | bytes 270336 | tf_op jit(solution)/shard_map/all_gather | solution.py:39
  637.2 9.2 all_to_all.173
  646.4 1.5 collective-permute-done.1
  647.9 5.3 fusion
  653.3 7.6 all_to_all.174
  660.9 0.6 broadcast_in_dim.97
  661.5 3.2 all-to-all-start.7
  664.6 5.2 all-to-all-done.7
  670.0 1.4 reduce-scatter.15.cloned.1.call-done
  671.4 0.8 multiply_reduce_fusion.1
  672.2 0.6 broadcast_in_dim.99
  672.8 3.2 all-to-all-start.8
  676.0 63.3 %psum.46 = f32[8,2]{0,1:T(2,128)S(1)} all-reduce(f32[8,2]{0,1:T(2,128)S(1)} %multiply_reduce_fusion.1), channel_id=1, replica_groups=mesh['site'=2,'wide'=32,'narrow'=4] {'wide'}, use_global_device_ids=true, to_apply=%region_14.15 | all-reduce | flops 16 | bytes 128 | tf_op jit(solution)/shard_map/psum | solution.py:36
  739.4 0.8 fusion.16
  740.2 0.6 broadcast_in_dim.100
  740.7 4.7 all-to-all-start.9
  745.5 62.4 %all_gather.22 = f32[8,8192]{1,0:T(8,128)} all-gather(f32[8,256]{1,0:T(8,128)S(1)} %fusion.16), channel_id=1, replica_groups=mesh['site'=2,'wide'=32,'narrow'=4] {'wide'}, dimensions={1}, use_global_device_ids=true | all-gather | bytes 270336 | tf_op jit(solution)/shard_map/all_gather | solution.py:39
  807.9 4.8 all-to-all-start.4
  812.9 6.5 all-to-all-done.4
  819.4 5.3 fusion.3
  824.7 0.6 broadcast_in_dim.101
  825.3 3.2 all-to-all-start.10
  828.6 5.1 all-to-all-done.10
  833.7 9.2 reduce-scatter.17.cloned.1.call-done
  842.9 0.8 multiply_reduce_fusion
  843.8 63.2 %psum.47 = f32[8,2]{0,1:T(2,128)S(1)} all-reduce(f32[8,2]{0,1:T(2,128)S(1)} %multiply_reduce_fusion), channel_id=1, replica_groups=mesh['site'=2,'wide'=32,'narrow'=4] {'wide'}, use_global_device_ids=true, to_apply=%region_17.18 | all-reduce | flops 16 | bytes 128 | tf_op jit(solution)/shard_map/psum | solution.py:36
  907.1 0.6 broadcast_in_dim.102
  907.7 3.2 all-to-all-start.11
  910.9 0.8 fusion.14
  911.7 62.4 %all_gather.23 = f32[8,8192]{1,0:T(8,128)} all-gather(f32[8,256]{1,0:T(8,128)S(1)} %fusion.14), channel_id=1, replica_groups=mesh['site'=2,'wide'=32,'narrow'=4] {'wide'}, dimensions={1}, use_global_device_ids=true | all-gather | bytes 270336 | tf_op jit(solution)/shard_map/all_gather | solution.py:39
  974.1 4.8 all-to-all-start.5
  979.0 0.5 broadcast_select_fusion.1
  979.5 6.1 all-to-all-done.5
  985.6 1.0 copy.12
  (48 shorter events, 1.9 us)
Async XLA Ops:
  7.2 325.3 %copy-start = (f32[32,1,2048]{2,1,0:T(1,128)S(1)}, f32[32,1,2048]{2,1,0:T(1,128)}, u32[]{:S(2)}) copy-start(f32[32,1,2048]{2,1,0:T(1,128)} %param.3) | copy-start | bytes 786436
  7.2 31.8 %reduce-scatter.7.cloned.1.call-start = ((), (), s32[]{:S(2)}) async-start(), calls=%async_computation.18 | async-start | bytes 81920 | tf_op jit(solution)/shard_map/reduce_scatter | solution.py:21
  12.7 182.3 %reduce-scatter.9.cloned.1.call-start = ((), (), s32[]{:S(2)}) async-start(), calls=%async_computation.19 | async-start | bytes 81920 | tf_op jit(solution)/shard_map/reduce_scatter | solution.py:21
  322.4 10.1 %all-to-all-start.1 = ((f32[8,4,2048]{2,0,1:T(8,128)}), f32[8,4,2048]{2,0,1:T(8,128)S(1)}, u32[]{:S(2)}, u32[]{:S(2)}) async-start(f32[8,4,2048]{2,0,1:T(8,128)} %bitcast.19), calls=%async_computation.3 | async-start | bytes 524288 | tf_op jit(solution)/shard_map/all_to_all | solution.py:45
  325.8 31.9 %reduce-scatter.11.cloned.1.call-start = ((), (), s32[]{:S(2)}) async-start(), calls=%async_computation.20 | async-start | bytes 81920 | tf_op jit(solution)/shard_map/reduce_scatter | solution.py:21
  332.6 1.6 collective-permute-start
  339.5 174.3 %reduce-scatter.13.cloned.1.call-start = ((), (), s32[]{:S(2)}) async-start(), calls=%async_computation.21 | async-start | bytes 81920 | tf_op jit(solution)/shard_map/reduce_scatter | solution.py:21
  495.6 175.8 %reduce-scatter.15.cloned.1.call-start = ((), (), s32[]{:S(2)}) async-start(), calls=%async_computation.22 | async-start | bytes 81920 | tf_op jit(solution)/shard_map/reduce_scatter | solution.py:21
  646.4 1.5 collective-permute-start.1
  661.5 8.4 all-to-all-start.7
  670.0 154.7 %collective-permute-start.2 = (f32[32]{0:T(128)S(1)}, f32[32]{0:T(128)S(1)}, u32[]{:S(2)}, u32[]{:S(2)}) collective-permute-start(f32[32]{0:T(128)S(1)} %select_n.125), channel_id=1, source_target_pairs={{0,128},{128,0},{1,129},{129,1},{2,130},{130,2},{3,131},{131,3},{4... | collective-permute-start | bytes 392 | tf_op jit(solution)/shard_map/ppermute | solution.py:14
  672.8 67.4 %all-to-all-start.8 = ((f32[8,4,1]{0,2,1:T(1,128)}), f32[8,4,1]{0,2,1:T(1,128)S(1)}, u32[]{:S(2)}, u32[]{:S(2)}) async-start(f32[8,4,1]{0,2,1:T(1,128)} %broadcast_in_dim.99), calls=%async_computation.14 | async-start | bytes 4096 | tf_op jit(solution)/shard_map/all_to_all | solution.py:46
  740.7 67.1 %all-to-all-start.9 = ((f32[8,4,1]{0,2,1:T(1,128)}), f32[8,4,1]{0,2,1:T(1,128)S(1)}, u32[]{:S(2)}, u32[]{:S(2)}) async-start(f32[8,4,1]{0,2,1:T(1,128)} %broadcast_in_dim.100), calls=%async_computation.15 | async-start | bytes 4096 | tf_op jit(solution)/shard_map/all_to_all | solution.py:46
  807.9 11.5 %all-to-all-start.4 = ((f32[8,4,2048]{2,0,1:T(8,128)}), f32[8,4,2048]{2,0,1:T(8,128)S(1)}, u32[]{:S(2)}, u32[]{:S(2)}) async-start(f32[8,4,2048]{2,0,1:T(8,128)} %bitcast.45), calls=%async_computation.9 | async-start | bytes 524288 | tf_op jit(solution)/shard_map/all_to_all | solution.py:45
  812.7 30.3 %reduce-scatter.17.cloned.1.call-start = ((), (), s32[]{:S(2)}) async-start(), calls=%async_computation.23 | async-start | bytes 81920 | tf_op jit(solution)/shard_map/reduce_scatter | solution.py:21
  825.3 8.4 all-to-all-start.10
  828.5 150.6 %collective-permute-start.3 = (f32[32]{0:T(128)S(1)}, f32[32]{0:T(128)S(1)}, u32[]{:S(2)}, u32[]{:S(2)}) collective-permute-start(f32[32]{0:T(128)S(1)} %add_add_fusion), channel_id=1, source_target_pairs={{0,128},{128,0},{1,129},{129,1},{2,130},{130,2},{3,131},{131,3},{4... | collective-permute-start | bytes 392 | tf_op jit(solution)/shard_map/ppermute | solution.py:14
  907.7 66.4 %all-to-all-start.11 = ((f32[8,4,1]{0,2,1:T(1,128)}), f32[8,4,1]{0,2,1:T(1,128)S(1)}, u32[]{:S(2)}, u32[]{:S(2)}) async-start(f32[8,4,1]{0,2,1:T(1,128)} %broadcast_in_dim.102), calls=%async_computation.17 | async-start | bytes 4096 | tf_op jit(solution)/shard_map/all_to_all | solution.py:46
  974.1 11.4 %all-to-all-start.5 = ((f32[8,4,2048]{2,0,1:T(8,128)}), f32[8,4,2048]{2,0,1:T(8,128)S(1)}, u32[]{:S(2)}, u32[]{:S(2)}) async-start(f32[8,4,2048]{2,0,1:T(8,128)} %bitcast.53), calls=%async_computation.11 | async-start | bytes 524288 | tf_op jit(solution)/shard_map/all_to_all | solution.py:45
Sparse Core Ops, SparseCore 0:
  12.8 26.1 reduce-scatter.6
  177.0 18.0 reduce-scatter.8
  339.6 18.0 reduce-scatter.10
  495.8 18.0 reduce-scatter.12
  653.4 18.0 reduce-scatter.14
  824.8 18.0 reduce-scatter.16
where the time goes:
time: 995 us; the launch traced here: 993 us
  blocking collectives  777 us (78%)
  waiting for transfers between devices  123 us (12%)
  matrix products  31.9 us (3%)
  starting transfers between devices  30.9 us (3%)
  between operations  14.3 us (1%)
  other arithmetic  11 us (1%)
    psum x6, blocking collectives, advance(): totals = lax.psum(squares, 'wide')  379 us
    all_gather x6, blocking collectives, advance(): lax.all_gather(raw_kept * scale[:, None], 'wide', axis=1, tiled=True)  362 us
    reduce_scatter x6, waiting for transfers between devices, advance(): lax.psum_scatter(jnp.einsum('bar,oard->bod', held, site_tensor, precision...  90.4 us
    dot_general x6, matrix products, advance(): jnp.einsum('bar,oard->bod', held, site_tensor, precision=highest, preferr...  31.9 us
    all_to_all x3, blocking collectives, advance(): lax.all_to_all(split_rows, 'narrow', split_axis=1, concat_axis=0, tiled=T...  27.6 us
  transfers between devices with their start and end apart: 18, of which 13 were waited for; matrix products, arithmetic and copies ran while one was open for 1% of the time, Pallas kernels for 0%

commit v1 on v0

--- a/solution.py
+++ b/solution.py
@@ -33,7 +33,7 @@
     local_choice = lax.dynamic_slice_in_dim(chosen, lax.axis_index("narrow") * share, share, 0)
     squares = jnp.sum(summed * summed, axis=2)
     raw_kept = jnp.where(local_choice[:, None] == 0, summed[:, 0, :], summed[:, 1, :])
-    totals = lax.psum(squares, "wide")
+    totals = jnp.sum(lax.all_gather(squares, "wide"), axis=0)
     both_mean = (totals[:, 0] + totals[:, 1]) / (2.0 * BOND)
     scale = lax.rsqrt(both_mean + epsilon)
     full_rows = lax.all_gather(raw_kept * scale[:, None], "wide", axis=1, tiled=True)

time: 995 us -> 817 us (0.82)
  blocking collectives: 777 us -> 589 us
  waiting for transfers between devices: 123 us -> 133 us
    psum x6 -> x0, blocking collectives: 379 us -> none  [advance(): totals = lax.psum(squares, 'wide')]
    all_gather x0 -> x6, blocking collectives: none -> 258 us  [advance(): totals = jnp.sum(lax.all_gather(squares, 'wide'), axis=0)]
    all_gather x6, blocking collectives: 362 us -> 296 us  [advance(): lax.all_gather(raw_kept * scale[:, None], 'wide', axis=1, tiled=True)]
    reduce_scatter x6, waiting for transfers between devices: 90.4 us -> 100 us  [advance(): lax.psum_scatter(jnp.einsum('bar,oard->bod', held, site_tensor, precision...]
  transfers between devices with their start and end apart: 18 -> 18, of which waited for: 13 -> 13; matrix products, arithmetic and copies ran while one was open for 1% -> 2% of each run, Pallas kernels for 0% -> 0%
where the time goes in v1:
time: 817 us; the launch traced here: 815 us
  blocking collectives  589 us (72%)
  waiting for transfers between devices  133 us (16%)
  matrix products  31.9 us (4%)
  starting transfers between devices  29.3 us (4%)
  between operations  14.3 us (2%)
  other arithmetic  11.3 us (1%)
    all_gather x6, blocking collectives, advance(): lax.all_gather(raw_kept * scale[:, None], 'wide', axis=1, tiled=True)  296 us
    all_gather x6, blocking collectives, advance(): totals = jnp.sum(lax.all_gather(squares, 'wide'), axis=0)  258 us
    reduce_scatter x6, waiting for transfers between devices, advance(): lax.psum_scatter(jnp.einsum('bar,oard->bod', held, site_tensor, precision...  100 us
    dot_general x6, matrix products, advance(): jnp.einsum('bar,oard->bod', held, site_tensor, precision=highest, preferr...  31.9 us
    all_to_all x3, blocking collectives, advance(): lax.all_to_all(split_rows, 'narrow', split_axis=1, concat_axis=0, tiled=T...  27.6 us
    all_to_all x3, waiting for transfers between devices, advance(): lax.all_to_all(split_rows, 'narrow', split_axis=1, concat_axis=0, tiled=T...  19.1 us
  transfers between devices with their start and end apart: 18, of which 13 were waited for; matrix products, arithmetic and copies ran while one was open for 2% of the time, Pallas kernels for 0%

profile of v1, /device:TPU:2, one launch (start us, length us, event | category | flops | bytes accessed | tf_op | source)
XLA Modules:
  0.0 814.7 jit_solution(17735559391198883577)
XLA Ops:
  7.2 5.4 fusion.2
  12.7 0.8 fusion.33
  13.7 25.3 %reduce-scatter.7.cloned.1.call-done = f32[8,2,256]{2,0,1:T(8,128)} async-done(((f32[32,2,256]{2,0,1:T(8,128)}), f32[8,2,256]{2,0,1:T(8,128)}) %reduce-scatter.7.cloned.1.call-update) | async-done | bytes 16400 | tf_op jit(solution)/shard_map/reduce_scatter | solution.py:21
  39.0 0.8 multiply_reduce_fusion.5
  39.8 43.0 %all-gather.6 = f32[32,8,2]{1,2,0:T(2,128)S(1)} all-gather(f32[1,8,2]{1,2,0:T(2,128)S(1)} %bitcast.193), channel_id=2, replica_groups=mesh['site'=2,'wide'=32,'narrow'=4] {'wide'}, dimensions={0}, use_global_device_ids=true | all-gather | bytes 2112 | tf_op jit(solution)/shard_map/all_gather | solution.py:36
  82.9 0.8 fusion.24
  83.7 47.4 %all_gather.56 = f32[8,8192]{1,0:T(8,128)S(1)} all-gather(f32[8,256]{1,0:T(8,128)S(1)} %fusion.24), channel_id=1, replica_groups=mesh['site'=2,'wide'=32,'narrow'=4] {'wide'}, dimensions={1}, use_global_device_ids=true | all-gather | bytes 270336 | tf_op jit(solution)/shard_map/all_gather | solution.py:39
  131.1 9.2 %all_to_all.171 = f32[8,4,2048]{2,0,1:T(8,128)S(1)} all-to-all(f32[8,4,2048]{2,0,1:T(8,128)S(1)} %bitcast.189), channel_id=1, replica_groups=mesh['site'=2,'wide'=32,'narrow'=4] {'narrow'}, dimensions={1} | all-to-all | bytes 524288 | tf_op jit(solution)/shard_map/all_to_all | solution.py:45
  140.3 5.3 fusion.5
  145.7 20.9 %reduce-scatter.9.cloned.1.call-done = f32[8,2,256]{2,0,1:T(8,128)} async-done(((f32[32,2,256]{2,0,1:T(8,128)}), f32[8,2,256]{2,0,1:T(8,128)}) %reduce-scatter.9.cloned.1.call-update) | async-done | bytes 16400 | tf_op jit(solution)/shard_map/reduce_scatter | solution.py:21
  166.6 0.8 multiply_reduce_fusion.4
  167.4 43.0 %all-gather.7 = f32[32,8,2]{1,2,0:T(2,128)S(1)} all-gather(f32[1,8,2]{1,2,0:T(2,128)S(1)} %bitcast.194), channel_id=3, replica_groups=mesh['site'=2,'wide'=32,'narrow'=4] {'wide'}, dimensions={0}, use_global_device_ids=true | all-gather | bytes 2112 | tf_op jit(solution)/shard_map/all_gather | solution.py:36
  210.5 0.8 fusion.22
  211.3 51.4 %all_gather.59 = f32[8,8192]{1,0:T(8,128)} all-gather(f32[8,256]{1,0:T(8,128)S(1)} %fusion.22), channel_id=1, replica_groups=mesh['site'=2,'wide'=32,'narrow'=4] {'wide'}, dimensions={1}, use_global_device_ids=true | all-gather | bytes 270336 | tf_op jit(solution)/shard_map/all_gather | solution.py:39
  262.7 3.4 all-to-all-start.1
  266.2 6.6 all-to-all-done.1
  272.8 0.1 bitcast_select_fusion.1
  273.0 1.5 collective-permute-done
  274.5 5.3 fusion.1
  280.0 20.9 %reduce-scatter.11.cloned.1.call-done = f32[8,2,256]{2,0,1:T(8,128)} async-done(((f32[32,2,256]{2,0,1:T(8,128)}), f32[8,2,256]{2,0,1:T(8,128)}) %reduce-scatter.11.cloned.1.call-update) | async-done | bytes 16400 | tf_op jit(solution)/shard_map/reduce_scatter | solution.py:21
  300.9 0.8 multiply_reduce_fusion.3
  301.7 43.0 %all-gather.8 = f32[32,8,2]{1,2,0:T(2,128)S(1)} all-gather(f32[1,8,2]{1,2,0:T(2,128)S(1)} %bitcast.195), channel_id=4, replica_groups=mesh['site'=2,'wide'=32,'narrow'=4] {'wide'}, dimensions={0}, use_global_device_ids=true | all-gather | bytes 2112 | tf_op jit(solution)/shard_map/all_gather | solution.py:36
  344.8 0.8 fusion.20
  345.6 47.4 %all_gather.62 = f32[8,8192]{1,0:T(8,128)S(1)} all-gather(f32[8,256]{1,0:T(8,128)S(1)} %fusion.20), channel_id=1, replica_groups=mesh['site'=2,'wide'=32,'narrow'=4] {'wide'}, dimensions={1}, use_global_device_ids=true | all-gather | bytes 270336 | tf_op jit(solution)/shard_map/all_gather | solution.py:39
  393.0 9.2 %all_to_all.172 = f32[8,4,2048]{2,0,1:T(8,128)S(1)} all-to-all(f32[8,4,2048]{2,0,1:T(8,128)S(1)} %bitcast.190), channel_id=1, replica_groups=mesh['site'=2,'wide'=32,'narrow'=4] {'narrow'}, dimensions={1} | all-to-all | bytes 524288 | tf_op jit(solution)/shard_map/all_to_all | solution.py:45
  402.2 5.3 fusion.4
  407.6 20.9 %reduce-scatter.13.cloned.1.call-done = f32[8,2,256]{2,0,1:T(8,128)} async-done(((f32[32,2,256]{2,0,1:T(8,128)}), f32[8,2,256]{2,0,1:T(8,128)}) %reduce-scatter.13.cloned.1.call-update) | async-done | bytes 16400 | tf_op jit(solution)/shard_map/reduce_scatter | solution.py:21
  428.5 0.8 multiply_reduce_fusion.2
  429.3 43.0 %all-gather.9 = f32[32,8,2]{1,2,0:T(2,128)S(1)} all-gather(f32[1,8,2]{1,2,0:T(2,128)S(1)} %bitcast.196), channel_id=5, replica_groups=mesh['site'=2,'wide'=32,'narrow'=4] {'wide'}, dimensions={0}, use_global_device_ids=true | all-gather | bytes 2112 | tf_op jit(solution)/shard_map/all_gather | solution.py:36
  472.4 0.8 fusion.18
  473.2 47.4 %all_gather.65 = f32[8,8192]{1,0:T(8,128)S(1)} all-gather(f32[8,256]{1,0:T(8,128)S(1)} %fusion.18), channel_id=1, replica_groups=mesh['site'=2,'wide'=32,'narrow'=4] {'wide'}, dimensions={1}, use_global_device_ids=true | all-gather | bytes 270336 | tf_op jit(solution)/shard_map/all_gather | solution.py:39
  520.6 9.2 %all_to_all.173 = f32[8,4,2048]{2,0,1:T(8,128)S(1)} all-to-all(f32[8,4,2048]{2,0,1:T(8,128)S(1)} %bitcast.191), channel_id=1, replica_groups=mesh['site'=2,'wide'=32,'narrow'=4] {'narrow'}, dimensions={1} | all-to-all | bytes 524288 | tf_op jit(solution)/shard_map/all_to_all | solution.py:45
  529.8 1.5 collective-permute-done.1
  531.4 5.3 fusion
  536.7 7.6 all_to_all.174
  544.3 0.6 broadcast_in_dim.97
  544.9 3.2 all-to-all-start.7
  548.1 5.3 all-to-all-done.7
  553.5 0.6 broadcast_in_dim.99
  554.0 3.2 all-to-all-start.8
  557.2 0.5 reduce-scatter.15.cloned.1.call-done
  557.7 0.8 multiply_reduce_fusion.1
  558.5 42.9 %all-gather.10 = f32[32,8,2]{1,2,0:T(2,128)S(1)} all-gather(f32[1,8,2]{1,2,0:T(2,128)S(1)} %bitcast.197), channel_id=6, replica_groups=mesh['site'=2,'wide'=32,'narrow'=4] {'wide'}, dimensions={0}, use_global_device_ids=true | all-gather | bytes 2112 | tf_op jit(solution)/shard_map/all_gather | solution.py:36
  601.6 0.8 fusion.16
  602.4 0.6 broadcast_in_dim.100
  602.9 3.2 all-to-all-start.9
  606.2 51.4 %all_gather.68 = f32[8,8192]{1,0:T(8,128)} all-gather(f32[8,256]{1,0:T(8,128)S(1)} %fusion.16), channel_id=1, replica_groups=mesh['site'=2,'wide'=32,'narrow'=4] {'wide'}, dimensions={1}, use_global_device_ids=true | all-gather | bytes 270336 | tf_op jit(solution)/shard_map/all_gather | solution.py:39
  657.6 4.8 all-to-all-start.4
  662.6 6.5 all-to-all-done.4
  669.0 5.3 fusion.3
  674.4 0.6 broadcast_in_dim.101
  675.0 3.2 all-to-all-start.10
  678.2 5.1 all-to-all-done.10
  683.5 11.9 %reduce-scatter.17.cloned.1.call-done = f32[8,2,256]{2,0,1:T(8,128)} async-done(((f32[32,2,256]{2,0,1:T(8,128)}), f32[8,2,256]{2,0,1:T(8,128)}) %reduce-scatter.17.cloned.1.call-update) | async-done | bytes 16400 | tf_op jit(solution)/shard_map/reduce_scatter | solution.py:21
  695.4 0.8 multiply_reduce_fusion
  696.2 43.0 %all-gather.11 = f32[32,8,2]{1,2,0:T(2,128)S(1)} all-gather(f32[1,8,2]{1,2,0:T(2,128)S(1)} %bitcast.198), channel_id=7, replica_groups=mesh['site'=2,'wide'=32,'narrow'=4] {'wide'}, dimensions={0}, use_global_device_ids=true | all-gather | bytes 2112 | tf_op jit(solution)/shard_map/all_gather | solution.py:36
  739.3 0.6 broadcast_in_dim.102
  739.9 3.2 all-to-all-start.11
  743.2 0.8 fusion.14
  743.9 51.4 %all_gather.71 = f32[8,8192]{1,0:T(8,128)} all-gather(f32[8,256]{1,0:T(8,128)S(1)} %fusion.14), channel_id=1, replica_groups=mesh['site'=2,'wide'=32,'narrow'=4] {'wide'}, dimensions={1}, use_global_device_ids=true | all-gather | bytes 270336 | tf_op jit(solution)/shard_map/all_gather | solution.py:39
  795.4 4.8 all-to-all-start.5
  800.2 0.5 broadcast_select_fusion.1
  800.8 6.1 all-to-all-done.5
  806.8 1.0 copy.12
  (54 shorter events, 2.2 us)
Async XLA Ops:
  7.2 265.6 %copy-start = (f32[32,1,2048]{2,1,0:T(1,128)S(1)}, f32[32,1,2048]{2,1,0:T(1,128)}, u32[]{:S(2)}) copy-start(f32[32,1,2048]{2,1,0:T(1,128)} %param.3) | copy-start | bytes 786436
  7.2 31.8 %reduce-scatter.7.cloned.1.call-start = ((), (), s32[]{:S(2)}) async-start(), calls=%async_computation.18 | async-start | bytes 81920 | tf_op jit(solution)/shard_map/reduce_scatter | solution.py:21
  12.7 153.9 %reduce-scatter.9.cloned.1.call-start = ((), (), s32[]{:S(2)}) async-start(), calls=%async_computation.19 | async-start | bytes 81920 | tf_op jit(solution)/shard_map/reduce_scatter | solution.py:21
  262.7 10.1 %all-to-all-start.1 = ((f32[8,4,2048]{2,0,1:T(8,128)}), f32[8,4,2048]{2,0,1:T(8,128)S(1)}, u32[]{:S(2)}, u32[]{:S(2)}) async-start(f32[8,4,2048]{2,0,1:T(8,128)} %bitcast.21), calls=%async_computation.3 | async-start | bytes 524288 | tf_op jit(solution)/shard_map/all_to_all | solution.py:45
  266.1 34.8 %reduce-scatter.11.cloned.1.call-start = ((), (), s32[]{:S(2)}) async-start(), calls=%async_computation.20 | async-start | bytes 81920 | tf_op jit(solution)/shard_map/reduce_scatter | solution.py:21
  272.9 1.6 collective-permute-start
  279.8 148.7 %reduce-scatter.13.cloned.1.call-start = ((), (), s32[]{:S(2)}) async-start(), calls=%async_computation.21 | async-start | bytes 81920 | tf_op jit(solution)/shard_map/reduce_scatter | solution.py:21
  407.5 150.2 %reduce-scatter.15.cloned.1.call-start = ((), (), s32[]{:S(2)}) async-start(), calls=%async_computation.22 | async-start | bytes 81920 | tf_op jit(solution)/shard_map/reduce_scatter | solution.py:21
  529.8 1.5 collective-permute-start.1
  544.9 8.4 %all-to-all-start.7 = ((f32[8,4,1]{0,2,1:T(1,128)}), f32[8,4,1]{0,2,1:T(1,128)S(1)}, u32[]{:S(2)}, u32[]{:S(2)}) async-start(f32[8,4,1]{0,2,1:T(1,128)} %broadcast_in_dim.97), calls=%async_computation.13 | async-start | bytes 4096 | tf_op jit(solution)/shard_map/all_to_all | solution.py:46
  553.4 120.9 %collective-permute-start.2 = (f32[32]{0:T(128)S(1)}, f32[32]{0:T(128)S(1)}, u32[]{:S(2)}, u32[]{:S(2)}) collective-permute-start(f32[32]{0:T(128)S(1)} %select_n.125), channel_id=1, source_target_pairs={{0,128},{128,0},{1,129},{129,1},{2,130},{130,2},{3,131},{131,3},{4... | collective-permute-start | bytes 392 | tf_op jit(solution)/shard_map/ppermute | solution.py:14
  554.0 48.3 %all-to-all-start.8 = ((f32[8,4,1]{0,2,1:T(1,128)}), f32[8,4,1]{0,2,1:T(1,128)S(1)}, u32[]{:S(2)}, u32[]{:S(2)}) async-start(f32[8,4,1]{0,2,1:T(1,128)} %broadcast_in_dim.99), calls=%async_computation.14 | async-start | bytes 4096 | tf_op jit(solution)/shard_map/all_to_all | solution.py:46
  602.9 54.7 %all-to-all-start.9 = ((f32[8,4,1]{0,2,1:T(1,128)}), f32[8,4,1]{0,2,1:T(1,128)S(1)}, u32[]{:S(2)}, u32[]{:S(2)}) async-start(f32[8,4,1]{0,2,1:T(1,128)} %broadcast_in_dim.100), calls=%async_computation.15 | async-start | bytes 4096 | tf_op jit(solution)/shard_map/all_to_all | solution.py:46
  657.6 11.4 %all-to-all-start.4 = ((f32[8,4,2048]{2,0,1:T(8,128)}), f32[8,4,2048]{2,0,1:T(8,128)S(1)}, u32[]{:S(2)}, u32[]{:S(2)}) async-start(f32[8,4,2048]{2,0,1:T(8,128)} %bitcast.50), calls=%async_computation.9 | async-start | bytes 524288 | tf_op jit(solution)/shard_map/all_to_all | solution.py:45
  662.4 33.1 %reduce-scatter.17.cloned.1.call-start = ((), (), s32[]{:S(2)}) async-start(), calls=%async_computation.23 | async-start | bytes 81920 | tf_op jit(solution)/shard_map/reduce_scatter | solution.py:21
  675.0 8.4 %all-to-all-start.10 = ((f32[8,4,1]{0,2,1:T(1,128)}), f32[8,4,1]{0,2,1:T(1,128)S(1)}, u32[]{:S(2)}, u32[]{:S(2)}) async-start(f32[8,4,1]{0,2,1:T(1,128)} %broadcast_in_dim.101), calls=%async_computation.16 | async-start | bytes 4096 | tf_op jit(solution)/shard_map/all_to_all | solution.py:46
  678.1 122.1 %collective-permute-start.3 = (f32[32]{0:T(128)S(1)}, f32[32]{0:T(128)S(1)}, u32[]{:S(2)}, u32[]{:S(2)}) collective-permute-start(f32[32]{0:T(128)S(1)} %add_add_fusion), channel_id=1, source_target_pairs={{0,128},{128,0},{1,129},{129,1},{2,130},{130,2},{3,131},{131,3},{4... | collective-permute-start | bytes 392 | tf_op jit(solution)/shard_map/ppermute | solution.py:14
  739.9 55.4 %all-to-all-start.11 = ((f32[8,4,1]{0,2,1:T(1,128)}), f32[8,4,1]{0,2,1:T(1,128)S(1)}, u32[]{:S(2)}, u32[]{:S(2)}) async-start(f32[8,4,1]{0,2,1:T(1,128)} %broadcast_in_dim.102), calls=%async_computation.17 | async-start | bytes 4096 | tf_op jit(solution)/shard_map/all_to_all | solution.py:46
  795.4 11.4 %all-to-all-start.5 = ((f32[8,4,2048]{2,0,1:T(8,128)}), f32[8,4,2048]{2,0,1:T(8,128)S(1)}, u32[]{:S(2)}, u32[]{:S(2)}) async-start(f32[8,4,2048]{2,0,1:T(8,128)} %bitcast.59), calls=%async_computation.11 | async-start | bytes 524288 | tf_op jit(solution)/shard_map/all_to_all | solution.py:45
Sparse Core Ops, SparseCore 0:
  12.8 26.1 reduce-scatter.6
  145.7 20.8 reduce-scatter.8
  279.9 20.9 reduce-scatter.10
  407.6 20.8 reduce-scatter.12
  536.8 20.8 reduce-scatter.14
  674.5 20.9 reduce-scatter.16
